TPU v7x, 512 devices: a whole 4x8x8 slice. The times are simulated.
512 devices in a mesh: row: 8 (over z), col: 16 (over y, core), vox: 4 (over x).
Axes of the slice: x: 4, y: 8, z: 8, core: 2. Of those that a mesh axis runs over, the one named last changes fastest.
Arguments:
- panel_top: bfloat16 [1024, 1024], P('row', ('col', 'vox')), may hold values from -0.059814453 to 0.059814453
- panel_low: bfloat16 [8192, 1024], P('row', ('col', 'vox')), may hold values from -1.1953125 to 1.1953125
- panel_next: bfloat16 [8192, 1024], P('row', ('col', 'vox')), may hold values from -1.1953125 to 1.1953125
- gram_rest: bfloat16 [8192, 8192], P('row', ('col', 'vox')), may hold values from -18 to 18
- inverses: bfloat16 [2, 1024, 1024], P(None, 'row'), as said below
- right_top: bfloat16 [2, 1024, 8192], P(None, None, ('col', 'vox')), may hold values from -1.796875 to 1.796875
- right_low: bfloat16 [8192, 8192], P('row', ('col', 'vox')), may hold values from -24 to 24
Outputs:
- factor: bfloat16 [2, 8192, 1024], P(None, 'row', ('col', 'vox'))
- solved: bfloat16 [2, 1024, 8192], P(None, None, ('col', 'vox'))
- trailing: float32 [8192, 8192], P('row', ('col', 'vox'))
- residual: float32 [8192, 8192], P('row', ('col', 'vox'))
Inputs may be any that keep to these rules, and one draw needn't show every extreme that they name: Each inverses[k] is lower triangular with diagonal entries from 1 to 2.
All inputs are finite; a program needn't handle non-finite values.
Results may differ from a plain program's by a relative error of at most 0.0057.
Values may be sent and summed in bfloat16 or wider, within the bound.
No kernel may reach another device: no remote copies, remote signals or barrier semaphores. Data moves between devices by JAX's collectives and lax.ppermute only.
A program may use at most 64 MiB of HBM per device.

v0:
```python
import jax
import jax.numpy as jnp
from jax import lax
from jax.sharding import PartitionSpec as P


def spread(block, axis, source):
    block = jnp.where(lax.axis_index(axis) == source, block, jnp.zeros_like(block))
    return lax.psum(block, axis)


def contract(left, right):
    return lax.dot_general(
        left, right, (((1,), (1,)), ((), ())), preferred_element_type=jnp.float32
    )


def per_device(panel_top, panel_low, panel_next, gram_rest, inverses, right_top, right_low):
    col_index = lax.axis_index(("col", "vox"))
    row_index = lax.axis_index("row")
    col_width = panel_low.shape[1]
    top_rows = panel_top.shape[0]
    low_rows = panel_low.shape[0]
    rest_cols = gram_rest.shape[1]
    root_row = col_index * rest_cols // low_rows
    whole_inverses = lax.all_gather(inverses, "row", axis=1, tiled=True)
    own_rows = lax.dynamic_slice_in_dim(whole_inverses, col_index * col_width, col_width, 1)
    rows_used = own_rows[0]
    own_top = contract(lax.all_gather(panel_top, ("col", "vox"), axis=1, tiled=True), rows_used)
    own_low = contract(lax.all_gather(panel_low, ("col", "vox"), axis=1, tiled=True), rows_used)
    first_top, first_low = (
        lax.all_gather(own_top.astype(jnp.bfloat16), ("col", "vox"), axis=1, tiled=True),
        lax.all_gather(own_low.astype(jnp.bfloat16), ("col", "vox"), axis=1, tiled=True),
    )
    outgoing = (
        lax.dynamic_slice_in_dim(
            first_top, col_index * col_width - root_row * top_rows, col_width, 0
        ),
        lax.dynamic_slice_in_dim(
            first_low, col_index * rest_cols - root_row * low_rows, rest_cols, 0
        ),
    )
    owner_top, owner_low = (
        spread(outgoing[0], "row", root_row),
        spread(outgoing[1], "row", root_row),
    )
    updated = (panel_next.astype(jnp.float32) - contract(first_low, owner_top)).astype(jnp.bfloat16)
    rows_used = own_rows[1]
    own_next = contract(lax.all_gather(updated, ("col", "vox"), axis=1, tiled=True), rows_used)
    second_low = lax.all_gather(own_next.astype(jnp.bfloat16), ("col", "vox"), axis=1, tiled=True)
    owner_next = spread(
        lax.dynamic_slice_in_dim(
            second_low, col_index * rest_cols - root_row * low_rows, rest_cols, 0
        ),
        "row",
        root_row,
    )
    trailing = (
        gram_rest.astype(jnp.float32)
        - contract(first_low, owner_low)
        - contract(second_low, owner_next)
    )
    first_solve = jnp.dot(
        whole_inverses[0], right_top[0], preferred_element_type=jnp.float32
    ).astype(jnp.bfloat16)
    top_slice = lax.dynamic_slice_in_dim(right_top[1], row_index * top_rows, top_rows, 0)
    top_part = (
        top_slice.astype(jnp.float32)
        - jnp.dot(first_top, first_solve, preferred_element_type=jnp.float32)
    ).astype(jnp.bfloat16)
    top_new = lax.all_gather(top_part, "row", axis=0, tiled=True)
    second_solve = jnp.dot(whole_inverses[1], top_new, preferred_element_type=jnp.float32).astype(
        jnp.bfloat16
    )
    residual = (
        right_low.astype(jnp.float32)
        - jnp.dot(first_low, first_solve, preferred_element_type=jnp.float32)
        - jnp.dot(second_low, second_solve, preferred_element_type=jnp.float32)
    )
    factor = jnp.stack(
        [
            lax.dynamic_slice_in_dim(first_low, col_index * col_width, col_width, 1),
            lax.dynamic_slice_in_dim(second_low, col_index * col_width, col_width, 1),
        ]
    )
    solved = jnp.stack([first_solve, second_solve])
    return (factor, solved, trailing, residual)


def solution(mesh):
    in_specs = (
        P("row", ("col", "vox")),
        P("row", ("col", "vox")),
        P("row", ("col", "vox")),
        P("row", ("col", "vox")),
        P(None, "row", None),
        P(None, None, ("col", "vox")),
        P("row", ("col", "vox")),
    )
    out_specs = (
        P(None, "row", ("col", "vox")),
        P(None, None, ("col", "vox")),
        P("row", ("col", "vox")),
        P("row", ("col", "vox")),
    )
    return jax.shard_map(
        per_device, mesh=mesh, in_specs=in_specs, out_specs=out_specs, check_vma=False
    )
```

profile of v0, /device:TPU:2, one launch (start us, length us, event | category | flops | bytes accessed | tf_op | source)
XLA Modules:
  0.0 587.9 jit_solution(6978349543570293704)
XLA Ops:
  7.2 0.0 copy-start.7
  7.2 0.0 all-gather.8.cloned.1.call-start
  7.2 0.7 all-gather.8.cloned.1.call-update
  7.9 0.0 all-gather.6.cloned.1.call-start
  8.0 0.7 all-gather.6.cloned.1.call-update
  8.7 0.0 copy-start.6
  8.7 0.0 all-gather.10.cloned.1.call-start
  8.7 88.6 %all-gather.8.cloned.1.call-done = bf16[1024,1024]{0,1:T(8,128)(2,1)} async-done(((bf16[1024,16]{0,1:T(8,128)(2,1)}), bf16[1024,1024]{0,1:T(8,128)(2,1)}) %all-gather.8.cloned.1.call-update) | async-done | bytes 2097168 | tf_op jit(solution)/shard_map/all_gather | solution.py:30
  97.4 59.5 %all-gather.6.cloned.1.call-done = bf16[2,1024,1024]{2,1,0:T(8,128)(2,1)} async-done(((bf16[2,128,1024]{2,1,0:T(8,128)(2,1)}), bf16[2,1024,1024]{2,1,0:T(8,128)(2,1)}) %all-gather.6.cloned.1.call-update) | async-done | bytes 4194320 | tf_op jit(solution)/shard_map/all_gather | solution.py:26
  156.9 2.6 fusion.6
  159.5 0.0 all-gather.10.cloned.1.call-update
  159.5 0.0 all-gather.12.cloned.1.call-start
  159.6 0.0 copy-done.7
  159.6 69.7 %all_gather.27 = bf16[128,1024]{0,1:T(8,128)(2,1)S(1)} all-gather(bf16[128,16]{0,1:T(8,128)(2,1)S(1)} %copy-done.7), channel_id=1, replica_groups=mesh['row'=8,'col'=16,'vox'=4] {'col','vox'}, dimensions={1}, use_global_device_ids=true | all-gather | bytes 266240 | tf_op jit(solution)/shard_map/all_gather | solution.py:29
  229.3 0.9 fusion.7
  230.2 66.4 %all_gather.28 = bf16[128,1024]{0,1:T(8,128)(2,1)S(1)} all-gather(bf16[128,16]{0,1:T(8,128)(2,1)S(1)} %fusion.7), channel_id=1, replica_groups=mesh['row'=8,'col'=16,'vox'=4] {'col','vox'}, dimensions={1}, use_global_device_ids=true | all-gather | bytes 266240 | tf_op jit(solution)/shard_map/all_gather | solution.py:32
  296.6 0.1 dynamic-slice_select_fusion.2
  296.8 31.6 %psum.21 = bf16[16,1024]{0,1:T(8,128)(2,1)S(1)} all-reduce(bf16[16,1024]{0,1:T(8,128)(2,1)S(1)} %dynamic-slice_select_fusion.2), channel_id=1, replica_groups=mesh['row'=8,'col'=16,'vox'=4] {'row'}, use_global_device_ids=true, to_apply=%region_0.1 | all-reduce | flops 16384 | bytes 65536 | tf_op jit(solution)/shard_map/psum | solution.py:9
  328.3 0.0 copy-start.4
  328.4 0.0 all-gather.10.cloned.1.call-done
  328.4 0.0 copy-done.6
  328.4 2.7 fusion.4
  331.1 0.0 all-gather.12.cloned.1.call-update
  331.1 0.0 all-gather.14.cloned.1.call-start
  331.2 80.5 %all-gather.12.cloned.1.call-done = bf16[1024,1024]{0,1:T(8,128)(2,1)} async-done(((bf16[1024,16]{0,1:T(8,128)(2,1)}), bf16[1024,1024]{0,1:T(8,128)(2,1)}) %all-gather.12.cloned.1.call-update) | async-done | bytes 2097168 | tf_op jit(solution)/shard_map/all_gather | solution.py:49
  411.7 2.6 convolution_convert_fusion
  414.3 0.0 all-gather.14.cloned.1.call-update
  414.3 0.0 all-reduce.3.cloned.1.call-start
  414.4 0.0 slice-start
  414.4 0.0 copy-done.4
  414.4 0.0 copy-start.8
  414.4 2.4 fusion.2
  416.9 0.0 slice-done
  416.9 0.3 fusion.5
  417.2 26.8 %all_gather.31 = bf16[1024,128]{1,0:T(8,128)(2,1)S(1)} all-gather(bf16[128,128]{1,0:T(8,128)(2,1)S(1)} %fusion.5), channel_id=1, replica_groups=mesh['row'=8,'col'=16,'vox'=4] {'row'}, dimensions={0}, use_global_device_ids=true | all-gather | bytes 294912 | tf_op jit(solution)/shard_map/all_gather | solution.py:71
  444.0 0.0 copy-done.8
  444.0 0.0 copy-start
  444.0 0.0 copy-start.2
  444.0 0.7 fusion.3
  444.7 0.8 pad_maximum_fusion
  445.5 0.0 copy-done
  445.6 0.8 dynamic-slice_select_fusion.1
  446.3 0.0 copy-done.2
  446.3 0.7 convolution_subtract_fusion.1
  447.1 48.9 %all-gather.14.cloned.1.call-done = bf16[1024,1024]{0,1:T(8,128)(2,1)} async-done(((bf16[1024,16]{0,1:T(8,128)(2,1)}), bf16[1024,1024]{0,1:T(8,128)(2,1)}) %all-gather.14.cloned.1.call-update) | async-done | bytes 2097168 | tf_op jit(solution)/shard_map/all_gather | solution.py:50
  496.0 1.7 dynamic-slice_select_fusion
  497.7 0.0 all-reduce.3.cloned.1.call-update
  497.7 0.8 dynamic-slice_bitcast_fusion.3
  498.4 0.6 pad_maximum_fusion.1
  499.1 0.0 copy-start.3
  499.1 3.2 convolution_subtract_fusion
  502.3 75.4 %all-reduce.3.cloned.1.call-done = (bf16[128,1024]{0,1:T(8,128)(2,1)}, bf16[128,1024]{0,1:T(8,128)(2,1)}) async-done(((bf16[128,1024]{0,1:T(8,128)(2,1)}, bf16[128,1024]{0,1:T(8,128)(2,1)}), (bf16[128,1024]{0,1:T(8,128)(2,1)}, bf16[128,1024]{0,1:T(8,128)(2,1)})) %all-reduce.3.cloned.1.call-update) | async-done | bytes 524304 | tf_op jit(solution)/shard_map/psum | solution.py:9
  577.6 0.0 copy-done.3
  577.6 0.0 copy-start.1
  577.6 0.0 copy-start.5
  577.6 1.8 convolution_subtract_fusion.3
  579.5 0.0 copy-done.1
  579.5 0.0 copy-done.5
  579.5 1.5 convolution_subtract_fusion.2
  (1 shorter events, 0.0 us)
Async XLA Ops:
  7.2 152.4 %copy-start.7 = (bf16[128,16]{0,1:T(8,128)(2,1)S(1)}, bf16[128,16]{0,1:T(8,128)(2,1)}, u32[]{:S(2)}) copy-start(bf16[128,16]{0,1:T(8,128)(2,1)} %param.7) | copy-start | bytes 12292
  7.2 90.2 %all-gather.8.cloned.1.call-start = ((), (), s32[]{:S(2)}) async-start(), calls=%async_computation.1 | async-start | bytes 2129920 | tf_op jit(solution)/shard_map/all_gather | solution.py:30
  7.9 149.0 %all-gather.6.cloned.1.call-start = ((), (), s32[]{:S(2)}) async-start(), calls=%async_computation | async-start | bytes 4718592 | tf_op jit(solution)/shard_map/all_gather | solution.py:26
  8.7 319.7 %copy-start.6 = (bf16[1024,16]{0,1:T(8,128)(2,1)S(1)}, bf16[1024,16]{0,1:T(8,128)(2,1)}, u32[]{:S(2)}) copy-start(bf16[1024,16]{0,1:T(8,128)(2,1)} %param.9) | copy-start | bytes 98308
  8.7 319.7 %all-gather.10.cloned.1.call-start = ((), (), s32[]{:S(2)}) async-start(), calls=%async_computation.2 | async-start | bytes 2129920 | tf_op jit(solution)/shard_map/all_gather | solution.py:33
  159.5 252.2 %all-gather.12.cloned.1.call-start = ((), (), s32[]{:S(2)}) async-start(), calls=%async_computation.3 | async-start | bytes 2129920 | tf_op jit(solution)/shard_map/all_gather | solution.py:49
  328.3 86.1 %copy-start.4 = (bf16[2,1024,128]{2,1,0:T(8,128)(2,1)S(1)}, bf16[2,1024,128]{2,1,0:T(8,128)(2,1)}, u32[]{:S(2)}) copy-start(bf16[2,1024,128]{2,1,0:T(8,128)(2,1)} %param.12) | copy-start | bytes 1572868
  331.1 164.9 %all-gather.14.cloned.1.call-start = ((), (), s32[]{:S(2)}) async-start(), calls=%async_computation.4 | async-start | bytes 2129920 | tf_op jit(solution)/shard_map/all_gather | solution.py:50
  414.3 163.3 %all-reduce.3.cloned.1.call-start = ((), (), s32[]{:S(2)}) async-start(), calls=%async_computation.5 | async-start | bytes 1048576 | tf_op jit(solution)/shard_map/psum | solution.py:9
  414.4 2.5 slice-start
  414.4 29.5 %copy-start.8 = (bf16[2,1024,1024]{2,1,0:T(8,128)(2,1)S(1)}, bf16[2,1024,1024]{2,1,0:T(8,128)(2,1)}, u32[]{:S(2)}) copy-start(bf16[2,1024,1024]{2,1,0:T(8,128)(2,1)} %all-gather.6.cloned.1.call-done) | copy-start | bytes 12582916
  444.0 1.6 copy-start
  444.0 2.4 copy-start.2
  499.1 78.6 %copy-start.3 = (bf16[1024,128]{1,0:T(8,128)(2,1)S(1)}, bf16[1024,128]{1,0:T(8,128)(2,1)}, u32[]{:S(2)}) copy-start(bf16[1024,128]{1,0:T(8,128)(2,1)} %param.10) | copy-start | bytes 786436
  577.6 1.8 copy-start.1
  577.6 1.9 copy-start.5
Sparse Core Ops, SparseCore 0:
  11.4 85.9 all-gather.7
  99.5 57.3 all-gather.5
  160.8 79.4 all-gather.9
  331.2 80.4 all-gather.11
  415.5 80.4 all-gather.13
  498.8 78.8 all-reduce.2
where the time goes:
time: 588 us
  waiting for transfers between devices  354 us (60%)
  blocking collectives  194 us (33%)
  matrix products  19.5 us (3%)
  between operations  14.3 us (2%)
    all_gather x1, waiting for transfers between devices, per_device(): lax.all_gather(panel_low, ('col', 'vox'), axis=1, tiled=True)  88.6 us
    all_gather x1, waiting for transfers between devices, per_device(): lax.all_gather(updated, ('col', 'vox'), axis=1, tiled=True)  80.5 us
    psum x1, waiting for transfers between devices, spread(): return lax.psum(block, axis)  75.4 us
    all_gather x1, blocking collectives, per_device(): lax.all_gather(panel_top, ('col', 'vox'), axis=1, tiled=True)  69.7 us
    all_gather x1, blocking collectives, per_device(): lax.all_gather(own_top.astype(jnp.bfloat16), ('col', 'vox'), axis=1, tile...  66.4 us
    all_gather x1, waiting for transfers between devices, per_device(): whole_inverses = lax.all_gather(inverses, 'row', axis=1, tiled=True)  59.5 us
    all_gather x1, waiting for transfers between devices, per_device(): lax.all_gather(own_next.astype(jnp.bfloat16), ('col', 'vox'), axis=1, til...  48.9 us
    psum x1, blocking collectives, spread(): return lax.psum(block, axis)  31.6 us
  transfers between devices with their start and end apart: 6, of which 5 were waited for; matrix products, arithmetic and copies ran while one was open for 2% of the time, Pallas kernels for 0%

commit v1 on v0

--- a/solution.py
+++ b/solution.py
@@ -23,7 +23,9 @@
     low_rows = panel_low.shape[0]
     rest_cols = gram_rest.shape[1]
     root_row = col_index * rest_cols // low_rows
-    whole_inverses = lax.all_gather(inverses, "row", axis=1, tiled=True)
+    whole_inverses = jnp.concatenate(
+        lax.all_to_all(jnp.stack([inverses] * lax.axis_size("row")), "row", 0, 0), axis=1
+    )
     own_rows = lax.dynamic_slice_in_dim(whole_inverses, col_index * col_width, col_width, 1)
     rows_used = own_rows[0]
     own_top = contract(lax.all_gather(panel_top, ("col", "vox"), axis=1, tiled=True), rows_used)

time: 588 us -> 552 us (0.939)
  waiting for transfers between devices: 354 us -> 298 us
  local copies, waits for them, and re-layouts: 0.85 us -> 12 us
  starting transfers between devices: 0.24 us -> 10.5 us
    all_to_all x0 -> x1, waiting for transfers between devices: none -> 95.5 us  [per_device(): lax.all_to_all(jnp.stack([inverses] * lax.axis_size('row')), 'row', 0, 0)]
    all_gather x1, waiting for transfers between devices: 88.6 us -> 0.01 us  [per_device(): lax.all_gather(panel_low, ('col', 'vox'), axis=1, tiled=True)]
    all_gather x1 -> x0, waiting for transfers between devices: 59.5 us -> none  [per_device(): whole_inverses = lax.all_gather(inverses, 'row', axis=1, tiled=True)]
    all_to_all x0 -> x1, starting transfers between devices: none -> 10.3 us  [per_device(): lax.all_to_all(jnp.stack([inverses] * lax.axis_size('row')), 'row', 0, 0)]
  transfers between devices with their start and end apart: 6 -> 6, of which waited for: 5 -> 4; matrix products, arithmetic and copies ran while one was open for 2% -> 3% of each run, Pallas kernels for 0% -> 0%
where the time goes in v1:
time: 552 us; the launch traced here: 551 us
  waiting for transfers between devices  298 us (54%)
  blocking collectives  195 us (35%)
  matrix products  17.7 us (3%)
  between operations  14 us (3%)
  local copies, waits for them, and re-layouts  12 us (2%)
  starting transfers between devices  10.5 us (2%)
    all_to_all x1, waiting for transfers between devices, per_device(): lax.all_to_all(jnp.stack([inverses] * lax.axis_size('row')), 'row', 0, 0)  95.5 us
    all_gather x1, waiting for transfers between devices, per_device(): lax.all_gather(updated, ('col', 'vox'), axis=1, tiled=True)  78.8 us
    psum x1, waiting for transfers between devices, spread(): return lax.psum(block, axis)  75.4 us
    all_gather x1, blocking collectives, per_device(): lax.all_gather(panel_top, ('col', 'vox'), axis=1, tiled=True)  68.8 us
    all_gather x1, blocking collectives, per_device(): lax.all_gather(own_top.astype(jnp.bfloat16), ('col', 'vox'), axis=1, tile...  67 us
    all_gather x1, waiting for transfers between devices, per_device(): lax.all_gather(own_next.astype(jnp.bfloat16), ('col', 'vox'), axis=1, til...  47.6 us
    psum x1, blocking collectives, spread(): return lax.psum(block, axis)  31.9 us
    all_gather x1, blocking collectives, per_device(): top_new = lax.all_gather(top_part, 'row', axis=0, tiled=True)  26.9 us
  transfers between devices with their start and end apart: 6, of which 4 were waited for; matrix products, arithmetic and copies ran while one was open for 3% of the time, Pallas kernels for 0%

profile of v1, /device:TPU:2, one launch (start us, length us, event | category | flops | bytes accessed | tf_op | source)
XLA Modules:
  0.0 550.9 jit_solution(15810987058612879693)
XLA Ops:
  7.2 3.5 stack.14
  10.7 10.3 %all-to-all-start = ((bf16[8,2,128,1024]{3,2,1,0:T(8,128)(2,1)}), bf16[8,2,128,1024]{3,2,1,0:T(8,128)(2,1)}, u32[]{:S(2)}, u32[]{:S(2)}) async-start(bf16[8,2,128,1024]{3,2,1,0:T(8,128)(2,1)} %stack.14), calls=%async_computation | async-start | bytes 8388608 | tf_op jit(solution)/shard_map/all_to_all | solution.py:27
  21.0 0.0 all-gather.5.cloned.1.call-start
  21.1 0.7 all-gather.5.cloned.1.call-update
  21.7 0.0 all-gather.7.cloned.1.call-start
  21.8 95.5 %all-to-all-done = bf16[8,2,128,1024]{3,2,1,0:T(8,128)(2,1)} async-done(((bf16[8,2,128,1024]{3,2,1,0:T(8,128)(2,1)}), bf16[8,2,128,1024]{3,2,1,0:T(8,128)(2,1)}, u32[]{:S(2)}, u32[]{:S(2)}) %all-to-all-start) | async-done | bytes 4194336 | tf_op jit(solution)/shard_map/all_to_all | solution.py:27
  117.3 4.7 copy.18
  122.0 0.0 copy-start.7
  122.0 0.0 copy-start.6
  122.0 0.0 all-gather.5.cloned.1.call-done
  122.0 2.6 fusion.2
  124.6 0.0 all-gather.7.cloned.1.call-update
  124.7 0.0 all-gather.9.cloned.1.call-start
  124.7 0.0 copy-done.7
  124.8 68.8 %all_gather.23 = bf16[128,1024]{0,1:T(8,128)(2,1)S(1)} all-gather(bf16[128,16]{0,1:T(8,128)(2,1)S(1)} %copy-done.7), channel_id=1, replica_groups=mesh['row'=8,'col'=16,'vox'=4] {'col','vox'}, dimensions={1}, use_global_device_ids=true | all-gather | bytes 266240 | tf_op jit(solution)/shard_map/all_gather | solution.py:31
  193.6 0.9 fusion.3
  194.5 67.0 %all_gather.24 = bf16[128,1024]{0,1:T(8,128)(2,1)S(1)} all-gather(bf16[128,16]{0,1:T(8,128)(2,1)S(1)} %fusion.3), channel_id=1, replica_groups=mesh['row'=8,'col'=16,'vox'=4] {'col','vox'}, dimensions={1}, use_global_device_ids=true | all-gather | bytes 266240 | tf_op jit(solution)/shard_map/all_gather | solution.py:34
  261.4 0.1 dynamic-slice_select_fusion.2
  261.6 31.9 %psum.21 = bf16[16,1024]{0,1:T(8,128)(2,1)S(1)} all-reduce(bf16[16,1024]{0,1:T(8,128)(2,1)S(1)} %dynamic-slice_select_fusion.2), channel_id=1, replica_groups=mesh['row'=8,'col'=16,'vox'=4] {'row'}, use_global_device_ids=true, to_apply=%region_0.1 | all-reduce | flops 16384 | bytes 65536 | tf_op jit(solution)/shard_map/psum | solution.py:9
  293.5 0.0 all-gather.7.cloned.1.call-done
  293.5 0.0 copy-done.6
  293.5 2.6 fusion
  296.2 0.0 all-gather.9.cloned.1.call-update
  296.2 0.0 all-gather.11.cloned.1.call-start
  296.2 78.8 %all-gather.9.cloned.1.call-done = bf16[1024,1024]{0,1:T(8,128)(2,1)} async-done(((bf16[1024,16]{0,1:T(8,128)(2,1)}), bf16[1024,1024]{0,1:T(8,128)(2,1)}) %all-gather.9.cloned.1.call-update) | async-done | bytes 2097168 | tf_op jit(solution)/shard_map/all_gather | solution.py:51
  375.0 2.6 convolution_convert_fusion.2
  377.6 0.0 all-gather.11.cloned.1.call-update
  377.6 0.0 all-reduce.3.cloned.1.call-start
  377.7 0.0 copy-start.4
  377.7 2.8 fusion.9
  380.5 0.0 slice-start
  380.5 0.0 copy-done.4
  380.5 0.7 convolution_convert_fusion.1
  381.2 0.2 slice-done
  381.4 0.3 fusion.1
  381.7 0.0 copy-start
  381.7 26.9 %all_gather.27 = bf16[1024,128]{1,0:T(8,128)(2,1)S(1)} all-gather(bf16[128,128]{1,0:T(8,128)(2,1)S(1)} %fusion.1), channel_id=1, replica_groups=mesh['row'=8,'col'=16,'vox'=4] {'row'}, dimensions={0}, use_global_device_ids=true | all-gather | bytes 294912 | tf_op jit(solution)/shard_map/all_gather | solution.py:73
  408.6 0.0 copy-start.2
  408.6 0.7 convolution_convert_fusion
  409.4 0.8 pad_maximum_fusion
  410.2 0.0 copy-done
  410.2 0.8 dynamic-slice_select_fusion.1
  411.0 0.0 copy-done.2
  411.0 0.7 convolution_subtract_fusion.1
  411.7 47.6 %all-gather.11.cloned.1.call-done = bf16[1024,1024]{0,1:T(8,128)(2,1)} async-done(((bf16[1024,16]{0,1:T(8,128)(2,1)}), bf16[1024,1024]{0,1:T(8,128)(2,1)}) %all-gather.11.cloned.1.call-update) | async-done | bytes 2097168 | tf_op jit(solution)/shard_map/all_gather | solution.py:52
  459.3 1.7 dynamic-slice_select_fusion
  461.0 0.0 all-reduce.3.cloned.1.call-update
  461.0 0.8 dynamic-slice_bitcast_fusion.3
  461.8 0.6 pad_maximum_fusion.1
  462.4 0.0 copy-start.3
  462.4 3.2 convolution_subtract_fusion
  465.6 75.4 %all-reduce.3.cloned.1.call-done = (bf16[128,1024]{0,1:T(8,128)(2,1)}, bf16[128,1024]{0,1:T(8,128)(2,1)}) async-done(((bf16[128,1024]{0,1:T(8,128)(2,1)}, bf16[128,1024]{0,1:T(8,128)(2,1)}), (bf16[128,1024]{0,1:T(8,128)(2,1)}, bf16[128,1024]{0,1:T(8,128)(2,1)})) %all-reduce.3.cloned.1.call-update) | async-done | bytes 524304 | tf_op jit(solution)/shard_map/psum | solution.py:9
  540.9 0.0 copy-done.3
  540.9 0.0 copy-start.1
  540.9 0.0 copy-start.5
  541.0 1.8 convolution_subtract_fusion.3
  542.8 0.0 copy-done.1
  542.8 0.0 copy-done.5
  542.8 1.5 convolution_subtract_fusion.2
  (1 shorter events, 0.0 us)
Async XLA Ops:
  10.7 106.6 %all-to-all-start = ((bf16[8,2,128,1024]{3,2,1,0:T(8,128)(2,1)}), bf16[8,2,128,1024]{3,2,1,0:T(8,128)(2,1)}, u32[]{:S(2)}, u32[]{:S(2)}) async-start(bf16[8,2,128,1024]{3,2,1,0:T(8,128)(2,1)} %stack.14), calls=%async_computation | async-start | bytes 8388608 | tf_op jit(solution)/shard_map/all_to_all | solution.py:27
  21.0 101.0 %all-gather.5.cloned.1.call-start = ((), (), s32[]{:S(2)}) async-start(), calls=%async_computation.1 | async-start | bytes 2129920 | tf_op jit(solution)/shard_map/all_gather | solution.py:32
  21.7 271.8 %all-gather.7.cloned.1.call-start = ((), (), s32[]{:S(2)}) async-start(), calls=%async_computation.2 | async-start | bytes 2129920 | tf_op jit(solution)/shard_map/all_gather | solution.py:35
  122.0 2.8 copy-start.7
  122.0 171.5 %copy-start.6 = (bf16[1024,16]{0,1:T(8,128)(2,1)S(1)}, bf16[1024,16]{0,1:T(8,128)(2,1)}, u32[]{:S(2)}) copy-start(bf16[1024,16]{0,1:T(8,128)(2,1)} %param.9) | copy-start | bytes 98308
  124.7 250.3 %all-gather.9.cloned.1.call-start = ((), (), s32[]{:S(2)}) async-start(), calls=%async_computation.3 | async-start | bytes 2129920 | tf_op jit(solution)/shard_map/all_gather | solution.py:51
  296.2 163.1 %all-gather.11.cloned.1.call-start = ((), (), s32[]{:S(2)}) async-start(), calls=%async_computation.4 | async-start | bytes 2129920 | tf_op jit(solution)/shard_map/all_gather | solution.py:52
  377.6 163.3 %all-reduce.3.cloned.1.call-start = ((), (), s32[]{:S(2)}) async-start(), calls=%async_computation.5 | async-start | bytes 1048576 | tf_op jit(solution)/shard_map/psum | solution.py:9
  377.7 2.8 copy-start.4
  380.5 1.0 slice-start
  381.7 28.5 %copy-start = (bf16[1024,1024]{0,1:T(8,128)(2,1)S(1)}, bf16[1024,1024]{0,1:T(8,128)(2,1)}, u32[]{:S(2)}) copy-start(bf16[1024,1024]{0,1:T(8,128)(2,1)} %all-gather.7.cloned.1.call-done) | copy-start | bytes 6291460
  408.6 2.3 copy-start.2
  462.4 78.5 %copy-start.3 = (bf16[1024,128]{1,0:T(8,128)(2,1)S(1)}, bf16[1024,128]{1,0:T(8,128)(2,1)}, u32[]{:S(2)}) copy-start(bf16[1024,128]{1,0:T(8,128)(2,1)} %param.10) | copy-start | bytes 786436
  540.9 1.8 copy-start.1
  540.9 1.9 copy-start.5
Sparse Core Ops, SparseCore 0:
  25.2 82.7 all-gather.4
  124.8 77.6 all-gather.6
  296.3 78.6 all-gather.8
  378.8 80.4 all-gather.10
  462.1 78.8 all-reduce.2
